TPU v7x, 128 devices: a whole 4x4x4 slice. The times are simulated.
128 devices in a mesh: expert: 64 (over z, y, x), dp: 2 (over core).
Axes of the slice: x: 4, y: 4, z: 4, core: 2. Of those that a mesh axis runs over, the one named last changes fastest.
Arguments:
- tokens: bfloat16 [8192, 2048], P(('expert', 'dp')), may hold values from -6 to 6
- grad_out: bfloat16 [8192, 2048], P(('expert', 'dp')), may hold values from -6 to 6
- expert_ids: int32 [8192, 8], P(('expert', 'dp')), may hold values from 0 to 63, all different within a row; in each aligned block of 64 rows (0 to 63, 64 to 127, ...) at most 12 rows name the same one
- router_weights: float32 [8192, 8], P(('expert', 'dp')), may hold values from 0.02 to 0.25
- codes_in: int32 [64, 2, 2048, 256], P('expert', None, 'dp'), may hold values from 0 to 4095
- codes_out: int32 [64, 256, 2048], P('expert', None, 'dp'), may hold values from 0 to 4095
- clip_in: float32 [64, 2, 2, 16, 768], P('expert'), may hold values from -1 to 3
- range_in: float32 [64, 2, 2, 16, 768], P('expert'), may hold values from 0.01 to 0.06
- clip_out: float32 [64, 2, 6, 2048], P('expert'), may hold values from -1 to 3
- range_out: float32 [64, 2, 6, 2048], P('expert'), may hold values from 0.018 to 0.1
Outputs:
- grad_tokens: bfloat16 [8192, 2048], P(('expert', 'dp'))
- grad_clip_in: float32 [64, 2, 2, 16, 768], P('expert', None, None, 'dp')
- grad_clip_out: float32 [64, 2, 6, 2048], P('expert', None, None, 'dp')
Inputs may be any that keep to these rules, and one draw needn't show every extreme that they name: `expert_ids`: each row names 8 different experts; among the rows of one device no expert is named by more than 12 rows, and in some device some expert is named by exactly 12 rows.
All inputs are finite; a program needn't handle non-finite values.
Results may differ from a plain program's by a relative error of at most 0.0082.
Values may be sent and summed in bfloat16 or wider, within the bound.
A program may use at most 128 MiB of HBM per device.

v0:
```python
import functools

import jax
import jax.numpy as jnp
from jax import lax
from jax.experimental import pallas as pl
from jax.experimental.pallas import tpu as pltpu
from jax.sharding import PartitionSpec as P

MESH = pl.DeviceIdType.MESH
D, FF, TOK = 2048, 768, 64
WIDTH = (640, 640, 768)
FIRST = (0, 640, 1280)
BF, F32, I32 = jnp.bfloat16, jnp.float32, jnp.int32
HI = lax.Precision.HIGHEST


def dot(a, b, da, db, **kw):
    return lax.dot_general(a, b, (((da,), (db,)), ((), ())), preferred_element_type=F32, **kw)


def iota(shape, dim):
    return lax.broadcasted_iota(I32, shape, dim)


def sigmoid(v):
    return 1.0 / (1.0 + jnp.exp(-v))


def down_blocks():
    out = []
    for k in range(3):
        for block in range(8):
            rows = range(block * 32, block * 32 + 32)
            groups = {}
            for r in rows:
                groups.setdefault((3 * r + k) // 128, []).append(r - block * 32)
            out.append((k, block * 32, [(g, min(v), max(v) + 1) for g, v in sorted(groups.items())]))
    return out


def kernel(
    tok, go, ids, rw, cin, cout, clin, rgin, clout, rgout,
    o_tok, o_in, o_out,
    posw, t4a, t4b, t4c, g4a, g4b, g4c, pw4,
    sta, stb, stc, ssa, ssb, ssc,
    x5, d5, g5, xeb, xec, deb, dec, geb, gec, ra, rb, rc, p4s,
    wgu, wd, upgu, logu, upo, loo,
    hid, ggu, fac, act, qa, qb, qc, ha, hb, hc,
    sbi, sbo, rbi, rbo,
    ag_s, ag_r, pw_s, pw_r, sl_s, sl_r, sl_l, rt_s, rt_r, rt_l, pt_s, pt_r, wt_s, wt_r, sm_s, sm_r,
):
    e, d = lax.axis_index("expert"), lax.axis_index("dp")
    z, y, x = e // 16, (e // 4) % 4, e % 4
    here = (x, y, z)
    t4, g4 = (t4a, t4b, t4c), (g4a, g4b, g4c)
    st, ss = (sta, stb, stc), (ssa, ssb, ssc)
    xe, de, ge = (None, xeb, xec), (None, deb, dec), (None, geb, gec)
    rr, part, got = (ra, rb, rc), (qa, qb, qc), (ha, hb, hc)
    cols = [pl.ds(FIRST[c], WIDTH[c]) for c in range(3)]

    def expert_at(zz, yy, xx):
        return zz * 16 + yy * 4 + xx

    def line_peer(c, k):
        s = (here[c] + k) % 4
        return s, (expert_at(z, y, s), expert_at(z, s, x), expert_at(s, y, x))[c]

    def plane_peer(c, o):
        a, b = o // 4, o % 4
        u, v = ((z, y), (z, x), (y, x))[c]
        u, v = (u + a) % 4, (v + b) % 4
        return u, v, (expert_at(u, v, x), expert_at(u, y, v), expert_at(z, u, v))[c]

    def main_rows(ref, c, u, v):
        if c == 0:
            return ref.at[u, v, :, :, cols[c]]
        if c == 1:
            return ref.at[u, :, v, :, cols[c]]
        return ref.at[pl.ds(0, 4), u, v, :, cols[c]]

    def extra_rows(ref, sides, c, u, v):
        if c == 0:
            return ref.at[4 + u // 2, (u % 2) * 2 + v // 2, pl.ds((v % 2) * 2, 2), :, cols[c]]
        return sides[c].at[u * 4 + v]

    def remote(src, dst, s, r, who, core):
        return pltpu.make_async_remote_copy(
            src_ref=src, dst_ref=dst, send_sem=s, recv_sem=r, device_id=(who, core), device_id_type=MESH
        )

    def wait_bytes(ref, sem):
        pltpu.make_async_copy(ref, ref, sem).wait()

    plane_me = (z * 4 + y, z * 4 + x, y * 4 + x)
    plane_uv = ((z, y), (z, x), (y, x))

    barrier = pltpu.get_barrier_semaphore()

    def greet(o, carry):
        pl.semaphore_signal(barrier, inc=1, device_id=((e + o) % 64, d), device_id_type=MESH)
        return carry

    lax.fori_loop(1, 64, greet, 0)
    pl.semaphore_signal(barrier, inc=1, device_id=(e, 1 - d), device_id_type=MESH)

    lane = iota((TOK, 128), 1)
    chosen = jnp.zeros((TOK, 128), F32)
    weight = jnp.zeros((TOK, 128), F32)
    for k in range(8):
        ident = ids[:, k : k + 1]
        chosen = chosen + jnp.where(lane == ident, 1.0, 0.0)
        weight = weight + jnp.where(lane == ident + 64, rw[:, k : k + 1], 0.0)
    lower_tri = jnp.where(iota((TOK, TOK), 0) > iota((TOK, TOK), 1), 1.0, 0.0).astype(BF)
    before = dot(lower_tri, chosen.astype(BF), 1, 0)
    posw[...] = jnp.where(chosen > 0.5, before, -64.0 * jnp.where(lane < 64, 1.0, 0.0)) + weight
    for c in range(3):
        pw4[c, here[c]] = posw[...]
        t4[c][here[c]] = tok[:, cols[c]]
        g4[c][here[c]] = go[:, cols[c]]

    pl.semaphore_wait(barrier, 64)

    for k in (2, 1, 3):
        for c in range(3):
            _, who = line_peer(c, k)
            remote(posw, pw4.at[c, here[c]], pw_s.at[c], pw_r.at[c], who, d).start()
            remote(tok.at[:, cols[c]], t4[c].at[here[c]], ag_s.at[0, c], ag_r.at[0, c], who, d).start()
    for k in (2, 1, 3):
        for c in range(3):
            _, who = line_peer(c, k)
            remote(go.at[:, cols[c]], g4[c].at[here[c]], ag_s.at[1, c], ag_r.at[1, c], who, d).start()

    perm = jnp.where(
        iota((FF, FF), 0) == 3 * (iota((FF, FF), 1) & 255) + (iota((FF, FF), 1) >> 8), 1.0, 0.0
    )
    for p in range(2):
        up = sigmoid(clin[p, 0]) * rgin[p, 0]
        lo = sigmoid(clin[p, 1]) * rgin[p, 1]
        upgu[:, p * FF : (p + 1) * FF] = dot(up, perm, 1, 0, precision=HI)
        logu[:, p * FF : (p + 1) * FF] = dot(lo, perm, 1, 0, precision=HI)
    upo[...] = sigmoid(clout[0]) * rgout[0]
    loo[...] = sigmoid(clout[1]) * rgout[1]

    def dequant_in(g, carry):
        up = upgu[pl.ds(d * 8 + g, 1), :]
        lo = logu[pl.ds(d * 8 + g, 1), :]
        step = (up + lo) / 15.0
        for p in range(2):
            words = cin[p, pl.ds(g * 128, 128), :]
            for k in range(3):
                c0 = p * FF + k * 256
                code = ((words >> (4 * k)) & 15).astype(F32)
                wgu[pl.ds(d * 1024 + g * 128, 128), c0 : c0 + 256] = (
                    code * step[:, c0 : c0 + 256] - lo[:, c0 : c0 + 256]
                ).astype(BF)
        return carry

    lax.fori_loop(0, 8, dequant_in, 0)
    half = pl.ds(pl.multiple_of(d * 1024, 1024), 1024)
    up_half, lo_half = upo[:, half], loo[:, half]
    step_half = (up_half + lo_half) / 15.0
    for k, r0, groups in down_blocks():
        code = ((cout[r0 : r0 + 32, :] >> (4 * k)) & 15).astype(F32)
        row = iota((32, 1024), 0)
        scale, shift = step_half[groups[0][0]][None], lo_half[groups[0][0]][None]
        for g, first, _ in groups[1:]:
            scale = jnp.where(row >= first, step_half[g][None], scale)
            shift = jnp.where(row >= first, lo_half[g][None], shift)
        wd[k * 256 + r0 : k * 256 + r0 + 32, half] = (code * scale - shift).astype(BF)

    other = 1 - d
    wgu_half = wgu.at[pl.ds(pl.multiple_of(d * 1024, 1024), 1024), :]
    wd_half = wd.at[:, half]
    remote(wgu_half, wgu_half, wt_s.at[0], wt_r.at[0], e, other).start()
    remote(wd_half, wd_half, wt_s.at[1], wt_r.at[1], e, other).start()

    def selector(c, first):
        q = iota((16, 48, 128), 0)
        u, v = q >> 2, q & 3
        target = (u * 16 + v * 4 + x, u * 16 + y * 4 + v, z * 16 + u * 4 + v)[c]
        return jnp.where(iota((16, 48, 128), 2) == target + first, 1.0, 0.0).reshape(768, 128)

    r = iota((16, 48, 256), 1)
    tail = r - 32
    wanted = jnp.where(r < 32, (r >> 3) * 16 + (r & 7), (tail >> 2) * 16 + 8 + (tail & 3))
    source = iota((16, 48, 256), 2) >> 6
    wanted = (wanted - 16 * source).astype(F32).reshape(768, 256)

    def send_slots(s, x_to, sides, c, t):
        def one(i, carry):
            o = jnp.where(i < 6, 10 + i, i - 5)
            u, v, who = plane_peer(c, o)
            q = u * 4 + v
            mu, mv = plane_uv[c]
            remote(s.at[q, pl.ds(0, 4)], main_rows(x_to, c, mu, mv), sl_s.at[t, c], sl_r.at[t, c], who, d).start()
            remote(s.at[q, pl.ds(4, 2)], extra_rows(x_to, sides, c, mu, mv), sl_s.at[t, c], sl_r.at[t, c], who, d).start()
            return carry

        lax.fori_loop(0, 15, one, 0)
        q = plane_me[c]
        mu, mv = plane_uv[c]
        pltpu.make_async_copy(s.at[q, pl.ds(0, 4)], main_rows(x_to, c, mu, mv), sl_l.at[t, c]).start()
        pltpu.make_async_copy(s.at[q, pl.ds(4, 2)], extra_rows(x_to, sides, c, mu, mv), sl_l.at[t, c]).start()

    slot_weights = []
    for c in range(3):
        wait_bytes(pw4.at[c, pl.ds(0, 3)], pw_r.at[c])
        wait_bytes(t4[c].at[pl.ds(0, 3)], ag_r.at[0, c])
        both = pw4[c].reshape(256, 128)
        found = dot(selector(c, 0).astype(BF), both.astype(BF), 1, 1)
        pick = jnp.where(found == wanted, 1.0, 0.0)
        p4s[c] = pick.astype(BF)
        slot_weights.append(
            jnp.sum(pick * dot(selector(c, 64), both, 1, 1, precision=HI), axis=1, keepdims=True)
        )
        rows = dot(p4s[c], t4[c][...].reshape(256, WIDTH[c]), 1, 0).astype(BF)
        st[c].reshape(768, WIDTH[c])[...] = rows
        send_slots(st[c], x5, xe, c, 0)
    for c in range(3):
        wait_bytes(g4[c].at[pl.ds(0, 3)], ag_r.at[1, c])
        rows = dot(p4s[c], g4[c][...].reshape(256, WIDTH[c]), 1, 0)
        ss[c].reshape(768, WIDTH[c])[...] = (slot_weights[c] * rows).astype(BF)
        send_slots(ss[c], d5, de, c, 1)

    def moved(v, c):
        if c == 1:
            return (v & 0xC3) | ((v >> 2) & 0x0C) | ((v << 2) & 0x30)
        return ((v & 0x0C) << 4) | ((v & 0xF0) >> 2) | (v & 3)

    def take_slots(s, x_to, sides, t):
        for c in range(3):
            wait_bytes(s[c].at[pl.ds(0, 15)], sl_r.at[t, c])
            wait_bytes(s[c].at[0], sl_l.at[t, c])
        flat = x_to.reshape(768, D)
        for c in (1, 2):
            order = jnp.where(iota((256, 256), 0) == moved(iota((256, 256), 1), c), 1.0, 0.0).astype(BF)
            flat[512:768, FIRST[c] : FIRST[c] + WIDTH[c]] = dot(
                order, sides[c][...].reshape(256, WIDTH[c]), 1, 0
            ).astype(BF)

    wait_bytes(wgu_half, wt_r.at[0])
    take_slots(st, x5, xe, 0)

    def forward(i, carry):
        rows = pl.ds(pl.multiple_of(i * 256, 256), 256)
        token_rows = x5.reshape(768, D)[rows, :]
        pre = dot(token_rows, wgu[...], 1, 0)
        gate, up = pre[:, :FF], pre[:, FF:]
        sig = sigmoid(gate)
        silu = gate * sig
        hid[rows, :] = (silu * up).astype(BF)
        act[rows, :] = silu
        fac[rows, :] = up * sig * (1.0 + gate * (1.0 - sig))
        return carry

    lax.fori_loop(0, 3, forward, 0)

    wait_bytes(wd_half, wt_r.at[1])
    take_slots(ss, d5, de, 1)

    def backward(i, carry):
        rows = pl.ds(pl.multiple_of(i * 256, 256), 256)
        grad_hidden = dot(d5.reshape(768, D)[rows, :], wd[...], 1, 1)
        ggu[rows, :FF] = (grad_hidden * fac[rows, :]).astype(BF)
        ggu[rows, FF:] = (grad_hidden * act[rows, :]).astype(BF)
        g5.reshape(768, D)[rows, :] = dot(ggu[rows, :], wgu[...], 1, 1).astype(BF)
        return carry

    lax.fori_loop(0, 3, backward, 0)

    for c in (1, 2):
        order = jnp.where(moved(iota((256, 256), 0), c) == iota((256, 256), 1), 1.0, 0.0).astype(BF)
        ge[c].reshape(256, WIDTH[c])[...] = dot(
            order, g5.reshape(768, D)[512:768, FIRST[c] : FIRST[c] + WIDTH[c]], 1, 0
        ).astype(BF)

    for c in range(3):
        def back(i, carry, c=c):
            o = jnp.where(i < 6, 10 + i, i - 5)
            u, v, who = plane_peer(c, o)
            to = rr[c].at[plane_me[c]]
            remote(main_rows(g5, c, u, v), to.at[pl.ds(0, 4)], rt_s.at[c], rt_r.at[c], who, d).start()
            remote(extra_rows(g5, ge, c, u, v), to.at[pl.ds(4, 2)], rt_s.at[c], rt_r.at[c], who, d).start()
            return carry

        lax.fori_loop(0, 15, back, 0)
        mu, mv = plane_uv[c]
        to = rr[c].at[plane_me[c]]
        pltpu.make_async_copy(main_rows(g5, c, mu, mv), to.at[pl.ds(0, 4)], rt_l.at[c]).start()
        pltpu.make_async_copy(extra_rows(g5, ge, c, mu, mv), to.at[pl.ds(4, 2)], rt_l.at[c]).start()

    def sums_in(j, carry):
        wide = pl.ds(pl.multiple_of(j * 512, 512), 512)
        grads = dot(x5.reshape(768, D)[:, wide], ggu[...], 0, 0)
        for g in range(4):
            low = logu[pl.ds(j * 4 + g, 1), :]
            grad = grads[g * 128 : (g + 1) * 128]
            value = wgu[pl.ds(j * 512 + g * 128, 128), :].astype(F32)
            at = pl.ds((j % 2) * 4 + g, 1)
            sbi[j // 2, 0, at, :] = jnp.sum(grad * (value + low), axis=0, keepdims=True)
            sbi[j // 2, 1, at, :] = jnp.sum(grad, axis=0, keepdims=True)
        return carry

    lax.fori_loop(0, 4, sums_in, 0)
    sbi_out = sbi.at[other]
    remote(sbi_out, rbi, sm_s.at[0], sm_r.at[0], e, other).start()

    def sums_out(j, carry):
        wide = pl.ds(pl.multiple_of(j * 512, 512), 512)
        grads = dot(hid[...], d5.reshape(768, D)[:, wide], 0, 0)
        low = loo[:, wide]
        total = [[jnp.zeros((1, 512), F32)] * 6, [jnp.zeros((1, 512), F32)] * 6]
        for k, r0, groups in down_blocks():
            grad = grads[k * 256 + r0 : k * 256 + r0 + 32]
            value = wd[k * 256 + r0 : k * 256 + r0 + 32, wide].astype(F32)
            row = iota((32, 512), 0)
            for g, first, last in groups:
                mine = grad
                if len(groups) > 1:
                    mine = jnp.where((row >= first) & (row < last), grad, 0.0)
                total[0][g] = total[0][g] + jnp.sum(mine * (value + low[g][None]), axis=0, keepdims=True)
                total[1][g] = total[1][g] + jnp.sum(mine, axis=0, keepdims=True)
        at = pl.ds(pl.multiple_of((j % 2) * 512, 512), 512)
        for t in range(2):
            for g in range(6):
                sbo[j // 2, t, g : g + 1, at] = total[t][g]
        return carry

    lax.fori_loop(0, 4, sums_out, 0)
    sbo_out = sbo.at[other]
    remote(sbo_out, rbo, sm_s.at[1], sm_r.at[1], e, other).start()

    for c in range(3):
        wait_bytes(rr[c].at[pl.ds(0, 15)], rt_r.at[c])
        wait_bytes(rr[c].at[0], rt_l.at[c])
        sums = dot(p4s[c], rr[c].reshape(768, WIDTH[c])[...], 0, 0).astype(BF)
        part[c][...] = sums.reshape(4, TOK, WIDTH[c])
        for k in (2, 1, 3):
            s, who = line_peer(c, k)
            remote(part[c].at[s], got[c].at[here[c]], pt_s.at[c], pt_r.at[c], who, d).start()

    wait_bytes(rbi, sm_r.at[0])
    share = pl.ds(pl.multiple_of(d * 8, 8), 8)
    upper_sum = (sbi[d, 0] + rbi[0]) / (upgu[share, :] + logu[share, :])
    lower_sum = upper_sum - (sbi[d, 1] + rbi[1])
    for p in range(2):
        for t, total in enumerate((upper_sum, lower_sum)):
            plain = dot(total[:, p * FF : (p + 1) * FF], perm, 1, 1, precision=HI)
            sig = sigmoid(clin[p, t, share, :])
            o_in[0, p, t] = plain * rgin[p, t, share, :] * sig * (1.0 - sig)
    wait_bytes(rbo, sm_r.at[1])
    span = upo[:, half] + loo[:, half]
    upper_out = (sbo[d, 0] + rbo[0])[:6] / span
    lower_out = upper_out - (sbo[d, 1] + rbo[1])[:6]
    for t, total in enumerate((upper_out, lower_out)):
        sig = sigmoid(clout[t, :, half])
        o_out[0, t] = total * rgout[t, :, half] * sig * (1.0 - sig)

    for c in range(3):
        wait_bytes(got[c].at[pl.ds(0, 3)], pt_r.at[c])
        total = part[c][here[c]].astype(F32)
        for k in (1, 2, 3):
            s, _ = line_peer(c, k)
            total = total + got[c][s].astype(F32)
        o_tok[:, cols[c]] = total.astype(BF)

    for c in range(3):
        wait_bytes(pw4.at[c, pl.ds(0, 3)], pw_s.at[c])
        wait_bytes(t4[c].at[pl.ds(0, 3)], ag_s.at[0, c])
        wait_bytes(g4[c].at[pl.ds(0, 3)], ag_s.at[1, c])
        for t, s in enumerate((st, ss)):
            wait_bytes(s[c].at[pl.ds(0, 15)], sl_s.at[t, c])
        wait_bytes(rr[c].at[pl.ds(0, 15)], rt_s.at[c])
        wait_bytes(got[c].at[pl.ds(0, 3)], pt_s.at[c])
    wait_bytes(wgu_half, wt_s.at[0])
    wait_bytes(wd_half, wt_s.at[1])
    wait_bytes(sbi_out, sm_s.at[0])
    wait_bytes(sbo_out, sm_s.at[1])


def body(tokens, grad_out, expert_ids, router_weights, codes_in, codes_out, clip_in, range_in, clip_out, range_out):
    def vm(*shape, t=BF):
        return pltpu.VMEM(shape, t)

    dma = pltpu.SemaphoreType.DMA
    scratch = [vm(TOK, 128, t=F32)]
    scratch += [vm(4, TOK, w) for w in WIDTH] * 2 + [vm(3, 4, TOK, 128, t=F32)]
    scratch += [vm(16, 6, 8, w) for w in WIDTH] * 2
    scratch += [vm(6, 4, 4, 8, D)] * 3
    scratch += [vm(16, 2, 8, w) for w in WIDTH[1:]] * 3
    scratch += [vm(16, 6, 8, w) for w in WIDTH] + [vm(3, 768, 256)]
    scratch += [vm(D, 2 * FF), vm(FF, D), vm(16, 2 * FF, t=F32), vm(16, 2 * FF, t=F32), vm(6, D, t=F32), vm(6, D, t=F32)]
    scratch += [vm(768, FF), vm(768, 2 * FF), vm(768, FF, t=F32), vm(768, FF, t=F32)]
    scratch += [vm(4, TOK, w) for w in WIDTH] * 2
    scratch += [vm(2, 2, 8, 2 * FF, t=F32), vm(2, 2, 8, 1024, t=F32), vm(2, 8, 2 * FF, t=F32), vm(2, 8, 1024, t=F32)]
    scratch += [dma((2, 3)), dma((2, 3)), dma((3,)), dma((3,)), dma((2, 3)), dma((2, 3)), dma((2, 3))]
    scratch += [dma((3,)), dma((3,)), dma((3,)), dma((3,)), dma((3,)), dma((2,)), dma((2,)), dma((2,)), dma((2,))]
    args = (
        tokens, grad_out, expert_ids, router_weights, codes_in[0], codes_out[0],
        clip_in[0], range_in[0], clip_out[0], range_out[0],
    )
    vmem = pl.BlockSpec(memory_space=pltpu.VMEM)
    return tuple(
        pl.pallas_call(
            kernel,
            out_shape=(
                jax.ShapeDtypeStruct((TOK, D), BF),
                jax.ShapeDtypeStruct((1, 2, 2, 8, FF), F32),
                jax.ShapeDtypeStruct((1, 2, 6, 1024), F32),
            ),
            in_specs=[vmem] * len(args),
            out_specs=(vmem,) * 3,
            scratch_shapes=scratch,
            compiler_params=pltpu.CompilerParams(
                collective_id=0, has_side_effects=True, vmem_limit_bytes=62 << 20
            ),
        )(*args)
    )


def solution(mesh):
    return jax.shard_map(
        body,
        mesh=mesh,
        in_specs=(
            P(("expert", "dp"), None),
            P(("expert", "dp"), None),
            P(("expert", "dp"), None),
            P(("expert", "dp"), None),
            P("expert", None, "dp", None),
            P("expert", None, "dp"),
            P("expert", None, None, None, None),
            P("expert", None, None, None, None),
            P("expert", None, None, None),
            P("expert", None, None, None),
        ),
        out_specs=(
            P(("expert", "dp"), None),
            P("expert", None, None, "dp", None),
            P("expert", None, None, "dp"),
        ),
        check_vma=False,
    )
```

profile of v0, /device:TPU:44, one launch (start us, length us, event | category | flops | bytes accessed | tf_op | source)
XLA Modules:
  0.0 139.4 jit_solution(15550051629288728683)
XLA Ops:
  0.6 1.4 copy.15.ids
  2.0 1.4 copy.16.rw
  3.4 1.8 %copy_bitcast_fusion = (f32[2,6,2048]{2,1,0:T(8,128)}, f32[2,6,2048]{2,1,0:T(8,128)}) fusion(f32[1,2,6,2048]{3,1,2,0:T(2,128)} %param.19, f32[1,2,6,2048]{3,1,2,0:T(2,128)} %param.18), kind=kLoop, calls=%fused_computation | loop fusion | bytes 393216 | tf_op jit(solution)/shard_map/squeeze | solution.py:401
  5.2 129.5 %shard_map.121 = (bf16[64,2048]{1,0:T(8,128)(2,1)}, f32[1,2,2,8,768]{4,3,2,1,0:T(8,128)}, f32[1,2,6,1024]{3,2,1,0:T(8,128)}) custom-call(bf16[64,2048]{1,0:T(8,128)(2,1)} %tok.1, bf16[64,2048]{1,0:T(8,128)(2,1)} %go.1, s32[64,8]{1,0:T(8,128)} %copy.15.ids, f32[64,8]{1,0:T(8,128)} %copy.16.rw, s32[2,1024,256]{2,1,0:T(8,128)} %bitcast.8, s32[256,1024]{1,0:T(8,128)} %bitcast.9, ...), custom_call_target="tpu_custom_call" | custom-call | tf_op jit(solution)/shard_map/pallas_call | solution.py:405
  134.7 1.5 %copy.17 = f32[1,2,6,1024]{3,1,2,0:T(2,128)} copy(f32[1,2,6,1024]{3,2,1,0:T(8,128)} %get-tuple-element.5) | data formatting | bytes 98304 | tf_op jit(solution)/shard_map/pallas_call | solution.py:405
  136.2 1.7 %copy.22 = bf16[64,2048]{1,0:T(8,128)(2,1)} copy(bf16[64,2048]{1,0:T(8,128)(2,1)} %get-tuple-element.11) | data formatting | bytes 524288
  137.8 1.5 %copy.23 = f32[1,2,2,8,768]{4,3,2,1,0:T(8,128)} copy(f32[1,2,2,8,768]{4,3,2,1,0:T(8,128)} %get-tuple-element.12) | data formatting | bytes 196608
where the time goes:
time: 140 us; the launch traced here: 139 us
  Pallas kernels  130 us (93%)
  local copies, waits for them, and re-layouts  9.23 us (7%)
    pallas_call x1, Pallas kernels, body(): pl.pallas_call(kernel, out_shape=(jax.ShapeDtypeStruct((TOK, D), BF), jax...  130 us
    unnamed x4, local copies, waits for them, and re-layouts  5.98 us

commit v1 on v0

v1 whole, which is shorter than its diff:
```python
import functools

import jax
import jax.numpy as jnp
from jax import lax
from jax.experimental import pallas as pl
from jax.experimental.pallas import tpu as pltpu
from jax.sharding import PartitionSpec as P

MESH = pl.DeviceIdType.MESH
D, FF, TOK = 2048, 768, 64
WIDTH = (640, 640, 768)
FIRST = (0, 640, 1280)
BF, F32, I32 = jnp.bfloat16, jnp.float32, jnp.int32
HI = lax.Precision.HIGHEST


def dot(a, b, da, db, **kw):
    return lax.dot_general(a, b, (((da,), (db,)), ((), ())), preferred_element_type=F32, **kw)


def iota(shape, dim):
    return lax.broadcasted_iota(I32, shape, dim)


def sigmoid(v):
    return 1.0 / (1.0 + jnp.exp(-v))


def down_blocks():
    out = []
    for k in range(3):
        for block in range(8):
            rows = range(block * 32, block * 32 + 32)
            groups = {}
            for r in rows:
                groups.setdefault((3 * r + k) // 128, []).append(r - block * 32)
            out.append((k, block * 32, [(g, min(v), max(v) + 1) for g, v in sorted(groups.items())]))
    return out


def split3(v):
    high = v.astype(BF)
    rest = v - high.astype(F32)
    mid = rest.astype(BF)
    low = (rest - mid.astype(F32)).astype(BF)
    return jnp.concatenate([high, mid, low], axis=0)


def join3(v):
    n = v.shape[0] // 3
    return (v[2 * n :] + v[n : 2 * n]) + v[:n]


def nibble_order():
    return jnp.where(
        iota((FF, FF), 0) == 3 * (iota((FF, FF), 1) & 255) + (iota((FF, FF), 1) >> 8), 1.0, 0.0
    ).astype(BF)


def kernel(
    tok, go, ids, rw, cin, cout, clin, rgin, clout, rgout,
    o_tok, o_in, o_out,
    posw, t4a, t4b, t4c, g4a, g4b, g4c, pw4,
    sma, smb, smc, dma_, dmb, dmc, sxa, sxb, sxc, dxa, dxb, dxc,
    x5, d5, g5, xeb, xec, deb, dec, geb, gec,
    rma, rmb, rmc, rxa, rxb, rxc, p4s,
    wgu, wd, upgu, logu, upo, loo, cinv, coutv,
    hid, ggu, fac, act, qa, qb, qc, ha, hb, hc,
    sbi, sbo, rbi, rbo,
    in_l, ag_s, ag_r, pw_s, pw_r, sl_s, sl_r, sl_l, rt_s, rt_r, rt_l, pt_s, pt_r, wt_s, wt_r, sm_s, sm_r,
):
    e, d = lax.axis_index("expert"), lax.axis_index("dp")
    z, y, x = e // 16, (e // 4) % 4, e % 4
    here = (x, y, z)
    t4, g4 = (t4a, t4b, t4c), (g4a, g4b, g4c)
    s_main, s_tail = ((sma, smb, smc), (dma_, dmb, dmc)), ((sxa, sxb, sxc), (dxa, dxb, dxc))
    xe, de, ge = (None, xeb, xec), (None, deb, dec), (None, geb, gec)
    r_main, r_tail = (rma, rmb, rmc), (rxa, rxb, rxc)
    part, got = (qa, qb, qc), (ha, hb, hc)
    cols = [pl.ds(FIRST[c], WIDTH[c]) for c in range(3)]

    def expert_at(zz, yy, xx):
        return zz * 16 + yy * 4 + xx

    def line_peer(c, k):
        s = (here[c] + k) % 4
        return s, (expert_at(z, y, s), expert_at(z, s, x), expert_at(s, y, x))[c]

    def plane_peer(c, o):
        a, b = o // 4, o % 4
        u, v = ((z, y), (z, x), (y, x))[c]
        u, v = (u + a) % 4, (v + b) % 4
        return u, v, (expert_at(u, v, x), expert_at(u, y, v), expert_at(z, u, v))[c]

    def main_rows(ref, c, u, v):
        if c == 0:
            return ref.at[u, v, :, :, cols[c]]
        if c == 1:
            return ref.at[u, :, v, :, cols[c]]
        return ref.at[pl.ds(0, 4), u, v, :, cols[c]]

    def tail_rows(ref, sides, c, u, v):
        if c == 0:
            return ref.at[4 + u // 2, (u % 2) * 2 + v // 2, pl.ds((v % 2) * 2, 2), :, cols[c]]
        return sides[c].at[u * 4 + v]

    def remote(src, dst, s, r, who, core):
        return pltpu.make_async_remote_copy(
            src_ref=src, dst_ref=dst, send_sem=s, recv_sem=r, device_id=(who, core), device_id_type=MESH
        )

    def wait_bytes(ref, sem):
        pltpu.make_async_copy(ref, ref, sem).wait()

    plane_me = (z * 4 + y, z * 4 + x, y * 4 + x)
    plane_uv = ((z, y), (z, x), (y, x))

    barrier = pltpu.get_barrier_semaphore()
    greeted = [(a, b, c) for a in range(4) for b in range(4) for c in range(4) if 0 in (a, b, c) and (a, b, c) != (0, 0, 0)]
    for a, b, c in greeted:
        who = expert_at((z + a) % 4, (y + b) % 4, (x + c) % 4)
        pl.semaphore_signal(barrier, inc=1, device_id=(who, d), device_id_type=MESH)
    pl.semaphore_signal(barrier, inc=1, device_id=(e, 1 - d), device_id_type=MESH)

    for c in range(3):
        pltpu.make_async_copy(tok.at[:, cols[c]], t4[c].at[here[c]], in_l.at[c]).start()
    codes_in = pltpu.make_async_copy(cin, cinv, in_l.at[6])
    codes_out = pltpu.make_async_copy(cout, coutv, in_l.at[7])
    codes_in.start()
    codes_out.start()
    for c in range(3):
        pltpu.make_async_copy(go.at[:, cols[c]], g4[c].at[here[c]], in_l.at[3 + c]).start()

    row = iota((128, TOK), 0)
    chosen = jnp.zeros((128, TOK), F32)
    weight = jnp.zeros((128, TOK), F32)
    for k in range(8):
        ident = ids[k : k + 1, :]
        chosen = chosen + jnp.where(row == ident, 1.0, 0.0)
        weight = weight + jnp.where(row == ident + 64, rw[k : k + 1, :], 0.0)
    earlier = jnp.where(iota((TOK, TOK), 0) < iota((TOK, TOK), 1), 1.0, 0.0).astype(BF)
    before = dot(chosen.astype(BF), earlier, 1, 0)
    rank = jnp.where(chosen > 0.5, before, jnp.where(row < 64, -64.0, 0.0)) + weight
    posw[...] = rank.T
    for c in range(3):
        pw4[c, here[c]] = posw[...]

    ends = [sigmoid(clin[p, t]) * rgin[p, t] for p in range(2) for t in range(2)]
    ends = join3(dot(split3(jnp.concatenate(ends, axis=0)), nibble_order(), 1, 0))
    for p in range(2):
        upgu[:, p * FF : (p + 1) * FF] = ends[p * 32 : p * 32 + 16]
        logu[:, p * FF : (p + 1) * FF] = ends[p * 32 + 16 : p * 32 + 32]
    for g in range(6):
        end = sigmoid(clout[g]) * rgout[g]
        upo[g : g + 1, :] = end[0:1]
        loo[g : g + 1, :] = end[1:2]

    codes_in.wait()
    codes_out.wait()

    def dequant_in(g, carry):
        up = upgu[pl.ds(d * 8 + g, 1), :]
        lo = logu[pl.ds(d * 8 + g, 1), :]
        step = (up + lo) / 15.0
        for p in range(2):
            words = cinv[p, pl.ds(g * 128, 128), :]
            for k in range(3):
                c0 = p * FF + k * 256
                code = ((words >> (4 * k)) & 15).astype(F32)
                wgu[pl.ds(d * 1024 + g * 128, 128), c0 : c0 + 256] = (
                    code * step[:, c0 : c0 + 256] - lo[:, c0 : c0 + 256]
                ).astype(BF)
        return carry

    lax.fori_loop(0, 8, dequant_in, 0)
    half = pl.ds(pl.multiple_of(d * 1024, 1024), 1024)
    up_half, lo_half = upo[:, half], loo[:, half]
    step_half = (up_half + lo_half) / 15.0
    for k, r0, groups in down_blocks():
        code = ((coutv[r0 : r0 + 32, :] >> (4 * k)) & 15).astype(F32)
        unit = iota((32, 1024), 0)
        scale, shift = step_half[groups[0][0]][None], lo_half[groups[0][0]][None]
        for g, first, _ in groups[1:]:
            scale = jnp.where(unit >= first, step_half[g][None], scale)
            shift = jnp.where(unit >= first, lo_half[g][None], shift)
        wd[k * 256 + r0 : k * 256 + r0 + 32, half] = (code * scale - shift).astype(BF)

    for c in range(3):
        wait_bytes(t4[c].at[here[c]], in_l.at[c])
        wait_bytes(g4[c].at[here[c]], in_l.at[3 + c])
    pl.semaphore_wait(barrier, len(greeted) + 1)

    for k in (2, 1, 3):
        for c in range(3):
            _, who = line_peer(c, k)
            remote(posw, pw4.at[c, here[c]], pw_s.at[c], pw_r.at[c], who, d).start()
    for k in (2, 1, 3):
        for c in range(3):
            _, who = line_peer(c, k)
            mine = t4[c].at[here[c]]
            remote(mine, mine, ag_s.at[0, c], ag_r.at[0, c], who, d).start()
    for k in (2, 1, 3):
        for c in range(3):
            _, who = line_peer(c, k)
            mine = g4[c].at[here[c]]
            remote(mine, mine, ag_s.at[1, c], ag_r.at[1, c], who, d).start()

    other = 1 - d
    wgu_half = wgu.at[pl.ds(pl.multiple_of(d * 1024, 1024), 1024), :]
    wd_half = wd.at[:, half]
    remote(wgu_half, wgu_half, wt_s.at[0], wt_r.at[0], e, other).start()
    remote(wd_half, wd_half, wt_s.at[1], wt_r.at[1], e, other).start()

    def selector(c, first):
        def rows(n):
            q = iota((16, n, 128), 0)
            u, v = q >> 2, q & 3
            target = (u * 16 + v * 4 + x, u * 16 + y * 4 + v, z * 16 + u * 4 + v)[c]
            return jnp.where(iota((16, n, 128), 2) == target + first, 1.0, 0.0).reshape(16 * n, 128)

        return jnp.concatenate([rows(32), rows(16)], axis=0).astype(BF)

    r = iota((16, 32, 256), 1)
    want_main = (r >> 3) * 16 + (r & 7) - 16 * (iota((16, 32, 256), 2) >> 6)
    r = iota((16, 16, 256), 1)
    want_tail = (r >> 2) * 16 + 8 + (r & 3) - 16 * (iota((16, 16, 256), 2) >> 6)
    wanted = jnp.concatenate([want_main.reshape(512, 256), want_tail.reshape(256, 256)], axis=0).astype(F32)

    def spread(c, t, src, to):
        def one(i, carry):
            o = jnp.where(i < 6, 10 + i, i - 5)
            u, v, who = plane_peer(c, o)
            remote(src.at[u * 4 + v], to, sl_s.at[t, c], sl_r.at[t, c], who, d).start()
            return carry

        lax.fori_loop(0, 15, one, 0)
        pltpu.make_async_copy(src.at[plane_me[c]], to, sl_l.at[t, c]).start()

    for c in range(3):
        wait_bytes(pw4.at[c, pl.ds(0, 3)], pw_r.at[c])
        found = dot(selector(c, 0), pw4[c].reshape(256, 128).astype(BF), 1, 1)
        p4s[c] = jnp.where(found == wanted, 1.0, 0.0).astype(BF)
    for c in range(3):
        wait_bytes(t4[c].at[pl.ds(0, 3)], ag_r.at[0, c])
        rows = dot(p4s[c, :512], t4[c][...].reshape(256, WIDTH[c]), 1, 0).astype(BF)
        s_main[0][c].reshape(512, WIDTH[c])[...] = rows
        spread(c, 0, s_main[0][c], main_rows(x5, c, *plane_uv[c]))
    slot_weights = []
    for c in range(3):
        parts = split3(pw4[c].reshape(256, 128))
        named = dot(selector(c, 64), parts, 1, 1)
        named = (named[:, 512:] + named[:, 256:512]) + named[:, :256]
        slot_weights.append(jnp.sum(p4s[c].astype(F32) * named, axis=1, keepdims=True))
    for c in range(3):
        wait_bytes(g4[c].at[pl.ds(0, 3)], ag_r.at[1, c])
        rows = dot(p4s[c, :512], g4[c][...].reshape(256, WIDTH[c]), 1, 0)
        s_main[1][c].reshape(512, WIDTH[c])[...] = (slot_weights[c][:512] * rows).astype(BF)
        spread(c, 1, s_main[1][c], main_rows(d5, c, *plane_uv[c]))
    for c in range(3):
        rows = dot(p4s[c, 512:], t4[c][...].reshape(256, WIDTH[c]), 1, 0).astype(BF)
        s_tail[0][c].reshape(256, WIDTH[c])[...] = rows
        spread(c, 2, s_tail[0][c], tail_rows(x5, xe, c, *plane_uv[c]))
    for c in range(3):
        rows = dot(p4s[c, 512:], g4[c][...].reshape(256, WIDTH[c]), 1, 0)
        s_tail[1][c].reshape(256, WIDTH[c])[...] = (slot_weights[c][512:] * rows).astype(BF)
        spread(c, 3, s_tail[1][c], tail_rows(d5, de, c, *plane_uv[c]))

    def moved(v, c):
        if c == 1:
            return (v & 0xC3) | ((v >> 2) & 0x0C) | ((v << 2) & 0x30)
        return ((v & 0x0C) << 4) | ((v & 0xF0) >> 2) | (v & 3)

    def arrived(t, src):
        for c in range(3):
            wait_bytes(src[c].at[pl.ds(0, 15)], sl_r.at[t, c])
            wait_bytes(src[c].at[0], sl_l.at[t, c])

    def order_tail(to, sides):
        for c in (1, 2):
            order = jnp.where(iota((256, 256), 0) == moved(iota((256, 256), 1), c), 1.0, 0.0).astype(BF)
            to.reshape(768, D)[512:768, FIRST[c] : FIRST[c] + WIDTH[c]] = dot(
                order, sides[c][...].reshape(256, WIDTH[c]), 1, 0
            ).astype(BF)

    def forward(i, carry):
        rows = pl.ds(pl.multiple_of(i * 256, 256), 256)
        token_rows = x5.reshape(768, D)[rows, :]
        pre = dot(token_rows, wgu[...], 1, 0)
        gate, up = pre[:, :FF], pre[:, FF:]
        sig = sigmoid(gate)
        silu = gate * sig
        hid[rows, :] = (silu * up).astype(BF)
        act[rows, :] = silu
        fac[rows, :] = up * sig * (1.0 + gate * (1.0 - sig))
        return carry

    def backward(i, carry):
        rows = pl.ds(pl.multiple_of(i * 256, 256), 256)
        grad_hidden = dot(d5.reshape(768, D)[rows, :], wd[...], 1, 1)
        ggu[rows, :FF] = (grad_hidden * fac[rows, :]).astype(BF)
        ggu[rows, FF:] = (grad_hidden * act[rows, :]).astype(BF)
        g5.reshape(768, D)[rows, :] = dot(ggu[rows, :], wgu[...], 1, 1).astype(BF)
        return carry

    def give_back(t, dst, rows_of):
        for c in range(3):
            to = dst[c].at[plane_me[c]]

            def one(i, carry, c=c, to=to):
                o = jnp.where(i < 6, 10 + i, i - 5)
                u, v, who = plane_peer(c, o)
                remote(rows_of(c, u, v), to, rt_s.at[t, c], rt_r.at[t, c], who, d).start()
                return carry

            lax.fori_loop(0, 15, one, 0)
            pltpu.make_async_copy(rows_of(c, *plane_uv[c]), to, rt_l.at[t, c]).start()

    wait_bytes(wgu_half, wt_r.at[0])
    wait_bytes(wd_half, wt_r.at[1])
    arrived(0, s_main[0])
    lax.fori_loop(0, 2, forward, 0)
    arrived(1, s_main[1])
    lax.fori_loop(0, 2, backward, 0)
    give_back(0, r_main, lambda c, u, v: main_rows(g5, c, u, v))

    arrived(2, s_tail[0])
    order_tail(x5, xe)
    lax.fori_loop(2, 3, forward, 0)
    arrived(3, s_tail[1])
    order_tail(d5, de)
    lax.fori_loop(2, 3, backward, 0)
    for c in (1, 2):
        order = jnp.where(moved(iota((256, 256), 0), c) == iota((256, 256), 1), 1.0, 0.0).astype(BF)
        ge[c].reshape(256, WIDTH[c])[...] = dot(
            order, g5.reshape(768, D)[512:768, FIRST[c] : FIRST[c] + WIDTH[c]], 1, 0
        ).astype(BF)
    give_back(1, r_tail, lambda c, u, v: tail_rows(g5, ge, c, u, v))

    def sums_in(j, carry):
        wide = pl.ds(pl.multiple_of(j * 512, 512), 512)
        grads = dot(x5.reshape(768, D)[:, wide], ggu[...], 0, 0)
        for g in range(4):
            low = logu[pl.ds(j * 4 + g, 1), :]
            grad = grads[g * 128 : (g + 1) * 128]
            value = wgu[pl.ds(j * 512 + g * 128, 128), :].astype(F32)
            at = pl.ds((j % 2) * 4 + g, 1)
            sbi[j // 2, 0, at, :] = jnp.sum(grad * (value + low), axis=0, keepdims=True)
            sbi[j // 2, 1, at, :] = jnp.sum(grad, axis=0, keepdims=True)
        return carry

    lax.fori_loop(0, 4, sums_in, 0)
    sbi_out = sbi.at[other]
    remote(sbi_out, rbi, sm_s.at[0], sm_r.at[0], e, other).start()

    def sums_out(j, carry):
        wide = pl.ds(pl.multiple_of(j * 512, 512), 512)
        grads = dot(hid[...], d5.reshape(768, D)[:, wide], 0, 0)
        low = loo[:, wide]
        total = [[jnp.zeros((1, 512), F32)] * 6, [jnp.zeros((1, 512), F32)] * 6]
        for k, r0, groups in down_blocks():
            grad = grads[k * 256 + r0 : k * 256 + r0 + 32]
            value = wd[k * 256 + r0 : k * 256 + r0 + 32, wide].astype(F32)
            unit = iota((32, 512), 0)
            for g, first, last in groups:
                mine = grad
                if len(groups) > 1:
                    mine = jnp.where((unit >= first) & (unit < last), grad, 0.0)
                total[0][g] = total[0][g] + jnp.sum(mine * (value + low[g][None]), axis=0, keepdims=True)
                total[1][g] = total[1][g] + jnp.sum(mine, axis=0, keepdims=True)
        at = pl.ds(pl.multiple_of((j % 2) * 512, 512), 512)
        for t in range(2):
            for g in range(6):
                sbo[j // 2, t, g : g + 1, at] = total[t][g]
        return carry

    lax.fori_loop(0, 4, sums_out, 0)
    sbo_out = sbo.at[other]
    remote(sbo_out, rbo, sm_s.at[1], sm_r.at[1], e, other).start()

    wait_bytes(rbi, sm_r.at[0])
    share = pl.ds(pl.multiple_of(d * 8, 8), 8)
    upper_sum = (sbi[d, 0] + rbi[0]) / (upgu[share, :] + logu[share, :])
    lower_sum = upper_sum - (sbi[d, 1] + rbi[1])
    totals = [total[:, p * FF : (p + 1) * FF] for p in range(2) for total in (upper_sum, lower_sum)]
    plain = join3(dot(split3(jnp.concatenate(totals, axis=0)), nibble_order(), 1, 1))
    for p in range(2):
        for t in range(2):
            sig = sigmoid(clin[p, t, share, :])
            total = plain[(p * 2 + t) * 8 : (p * 2 + t) * 8 + 8]
            o_in[0, p, t] = total * rgin[p, t, share, :] * sig * (1.0 - sig)
    wait_bytes(rbo, sm_r.at[1])
    span = upo[:, half] + loo[:, half]
    upper_out = (sbo[d, 0] + rbo[0])[:6] / span
    lower_out = upper_out - (sbo[d, 1] + rbo[1])[:6]
    for g in range(6):
        sig = sigmoid(clout[g, :, half])
        total = jnp.concatenate([upper_out[g : g + 1], lower_out[g : g + 1]], axis=0)
        o_out[g] = total * rgout[g, :, half] * sig * (1.0 - sig)

    sums = []
    for c in range(3):
        wait_bytes(s_main[0][c].at[pl.ds(0, 15)], rt_r.at[0, c])
        wait_bytes(s_main[0][c].at[0], rt_l.at[0, c])
        sums.append(dot(p4s[c, :512], r_main[c].reshape(512, WIDTH[c])[...], 0, 0))
    for c in range(3):
        wait_bytes(s_tail[0][c].at[pl.ds(0, 15)], rt_r.at[1, c])
        wait_bytes(s_tail[0][c].at[0], rt_l.at[1, c])
        total = sums[c] + dot(p4s[c, 512:], r_tail[c].reshape(256, WIDTH[c])[...], 0, 0)
        part[c][...] = total.astype(BF).reshape(4, TOK, WIDTH[c])
        for k in (2, 1, 3):
            s, who = line_peer(c, k)
            remote(part[c].at[s], got[c].at[here[c]], pt_s.at[c], pt_r.at[c], who, d).start()
    for c in range(3):
        wait_bytes(got[c].at[pl.ds(0, 3)], pt_r.at[c])
        total = part[c][here[c]].astype(F32)
        for k in (1, 2, 3):
            s, _ = line_peer(c, k)
            total = total + got[c][s].astype(F32)
        o_tok[:, cols[c]] = total.astype(BF)

    for c in range(3):
        wait_bytes(pw4.at[c, pl.ds(0, 3)], pw_s.at[c])
        wait_bytes(t4[c].at[pl.ds(0, 3)], ag_s.at[0, c])
        wait_bytes(g4[c].at[pl.ds(0, 3)], ag_s.at[1, c])
        for t in range(2):
            wait_bytes(s_main[t][c].at[pl.ds(0, 15)], sl_s.at[t, c])
            wait_bytes(s_tail[t][c].at[pl.ds(0, 15)], sl_s.at[2 + t, c])
        wait_bytes(s_main[0][c].at[pl.ds(0, 15)], rt_s.at[0, c])
        wait_bytes(s_tail[0][c].at[pl.ds(0, 15)], rt_s.at[1, c])
        wait_bytes(got[c].at[pl.ds(0, 3)], pt_s.at[c])
    wait_bytes(wgu_half, wt_s.at[0])
    wait_bytes(wd_half, wt_s.at[1])
    wait_bytes(sbi_out, sm_s.at[0])
    wait_bytes(sbo_out, sm_s.at[1])


def hand_out(a, b, c, to_a, to_b, to_c):
    to_a[...] = a[...]
    to_b[...] = b[...]
    to_c[...] = c[...]


def body(tokens, grad_out, expert_ids, router_weights, codes_in, codes_out, clip_in, range_in, clip_out, range_out):
    def vm(*shape, t=BF):
        return pltpu.VMEM(shape, t)

    dma = pltpu.SemaphoreType.DMA
    scratch = [vm(TOK, 128, t=F32)]
    scratch += [vm(4, TOK, w) for w in WIDTH] * 2 + [vm(3, 4, TOK, 128, t=F32)]
    scratch += [vm(16, 4, 8, w) for w in WIDTH] * 2 + [vm(16, 2, 8, w) for w in WIDTH] * 2
    scratch += [vm(6, 4, 4, 8, D)] * 3
    scratch += [vm(16, 2, 8, w) for w in WIDTH[1:]] * 3
    scratch += [vm(16, 4, 8, w) for w in WIDTH] + [vm(16, 2, 8, w) for w in WIDTH] + [vm(3, 768, 256)]
    scratch += [vm(D, 2 * FF), vm(FF, D), vm(16, 2 * FF, t=F32), vm(16, 2 * FF, t=F32), vm(6, D, t=F32), vm(6, D, t=F32)]
    scratch += [vm(2, 1024, 256, t=I32), vm(256, 1024, t=I32)]
    scratch += [vm(768, FF), vm(768, 2 * FF), vm(768, FF, t=F32), vm(768, FF, t=F32)]
    scratch += [vm(4, TOK, w) for w in WIDTH] * 2
    scratch += [vm(2, 2, 8, 2 * FF, t=F32), vm(2, 2, 8, 1024, t=F32), vm(2, 8, 2 * FF, t=F32), vm(2, 8, 1024, t=F32)]
    scratch += [dma((8,)), dma((2, 3)), dma((2, 3)), dma((3,)), dma((3,)), dma((4, 3)), dma((4, 3)), dma((4, 3))]
    scratch += [dma((2, 3)), dma((2, 3)), dma((2, 3)), dma((3,)), dma((3,)), dma((2,)), dma((2,)), dma((2,)), dma((2,))]
    args = (
        tokens, grad_out, expert_ids.T, router_weights.T, codes_in[0], codes_out[0],
        clip_in[0], range_in[0], clip_out[0].transpose(1, 0, 2), range_out[0].transpose(1, 0, 2),
    )
    vmem, anywhere = pl.BlockSpec(memory_space=pltpu.VMEM), pl.BlockSpec(memory_space=pl.ANY)
    results = (
        jax.ShapeDtypeStruct((TOK, D), BF),
        jax.ShapeDtypeStruct((1, 2, 2, 8, FF), F32),
        jax.ShapeDtypeStruct((6, 2, 1024), F32),
    )
    found = pl.pallas_call(
        kernel,
        out_shape=results,
        in_specs=[anywhere, anywhere, vmem, vmem, anywhere, anywhere, vmem, vmem, vmem, vmem],
        out_specs=(vmem,) * 3,
        scratch_shapes=scratch,
        compiler_params=pltpu.CompilerParams(collective_id=0, has_side_effects=True, vmem_limit_bytes=62 << 20),
    )(*args)
    grad_tokens, grad_in, grad_out_clip = pl.pallas_call(
        hand_out, out_shape=results, in_specs=[vmem] * 3, out_specs=(vmem,) * 3
    )(*found)
    return grad_tokens, grad_in, grad_out_clip.transpose(1, 0, 2)[None]


def solution(mesh):
    return jax.shard_map(
        body,
        mesh=mesh,
        in_specs=(
            P(("expert", "dp"), None),
            P(("expert", "dp"), None),
            P(("expert", "dp"), None),
            P(("expert", "dp"), None),
            P("expert", None, "dp", None),
            P("expert", None, "dp"),
            P("expert", None, None, None, None),
            P("expert", None, None, None, None),
            P("expert", None, None, None),
            P("expert", None, None, None),
        ),
        out_specs=(
            P(("expert", "dp"), None),
            P("expert", None, None, "dp", None),
            P("expert", None, None, "dp"),
        ),
        check_vma=False,
    )
```

time: 140 us -> 103 us (0.74)
  the two profiles are of different devices: /device:TPU:44 before, /device:TPU:0 now
where the time goes in v1:
time: 103 us; the launch traced here: 102 us
  Pallas kernels  101 us (98%)
    pallas_call x1, Pallas kernels, body(): pl.pallas_call(kernel, out_shape=results, in_specs=[anywhere, anywhere, v...  99.2 us

profile of v1, /device:TPU:0, one launch (start us, length us, event | category | flops | bytes accessed | tf_op | source)
XLA Modules:
  0.0 101.6 jit_solution(188748115143357620)
XLA Ops:
  0.6 99.2 %shard_map.121 = (bf16[64,2048]{1,0:T(8,128)(2,1)}, f32[1,2,2,8,768]{4,3,2,1,0:T(8,128)}, f32[6,2,1024]{2,1,0:T(2,128)}) custom-call(bf16[64,2048]{1,0:T(8,128)(2,1)} %tok.1, bf16[64,2048]{1,0:T(8,128)(2,1)} %go.1, s32[8,64]{1,0:T(8,128)} %bitcast.21, f32[8,64]{1,0:T(8,128)} %bitcast.22, s32[2,1024,256]{2,1,0:T(8,128)} %bitcast.15, s32[256,1024]{1,0:T(8,128)} %bitcast.16, ...), custom_call_target="tpu_custom_call" | custom-call | tf_op jit(solution)/shard_map/pallas_call | solution.py:472
  99.8 1.8 %shard_map.122 = (bf16[64,2048]{1,0:T(8,128)(2,1)}, f32[1,2,2,8,768]{4,3,2,1,0:T(8,128)}, f32[6,2,1024]{2,1,0:T(2,128)}) custom-call(bf16[64,2048]{1,0:T(8,128)(2,1)} %get-tuple-element.9.a, f32[1,2,2,8,768]{4,3,2,1,0:T(8,128)} %get-tuple-element.10.b, f32[6,2,1024]{2,1,0:T(2,128)} %get-tuple-element.11.c), custom_call_target="tpu_custom_call" | custom-call | tf_op jit(solution)/shard_map/pallas_call | solution.py:480

commit v2 on v1

--- a/solution.py
+++ b/solution.py
@@ -9,8 +9,8 @@
 
 MESH = pl.DeviceIdType.MESH
 D, FF, TOK = 2048, 768, 64
-WIDTH = (640, 640, 768)
-FIRST = (0, 640, 1280)
+WIDTH = ((640, 640, 768), (640, 768, 640), (768, 640, 640))
+FIRST = ((0, 640, 1280), (0, 640, 1408), (0, 768, 1408))
 BF, F32, I32 = jnp.bfloat16, jnp.float32, jnp.int32
 HI = lax.Precision.HIGHEST
 
@@ -61,11 +61,11 @@
 def kernel(
     tok, go, ids, rw, cin, cout, clin, rgin, clout, rgout,
     o_tok, o_in, o_out,
-    posw, t4a, t4b, t4c, g4a, g4b, g4c, pw4,
+    tab, t4a, t4b, t4c, g4a, g4b, g4c, pw4,
     sma, smb, smc, dma_, dmb, dmc, sxa, sxb, sxc, dxa, dxb, dxc,
     x5, d5, g5, xeb, xec, deb, dec, geb, gec,
     rma, rmb, rmc, rxa, rxb, rxc, p4s,
-    wgu, wd, upgu, logu, upo, loo, cinv, coutv,
+    wgu, wd, upgu, logu, upo, loo, cinv, coutv, idv, rwv, clinv, rginv, cloutv, rgoutv,
     hid, ggu, fac, act, qa, qb, qc, ha, hb, hc,
     sbi, sbo, rbi, rbo,
     in_l, ag_s, ag_r, pw_s, pw_r, sl_s, sl_r, sl_l, rt_s, rt_r, rt_l, pt_s, pt_r, wt_s, wt_r, sm_s, sm_r,
@@ -78,7 +78,7 @@
     xe, de, ge = (None, xeb, xec), (None, deb, dec), (None, geb, gec)
     r_main, r_tail = (rma, rmb, rmc), (rxa, rxb, rxc)
     part, got = (qa, qb, qc), (ha, hb, hc)
-    cols = [pl.ds(FIRST[c], WIDTH[c]) for c in range(3)]
+    cols = [[pl.ds(FIRST[t][c], WIDTH[t][c]) for c in range(3)] for t in range(3)]
 
     def expert_at(zz, yy, xx):
         return zz * 16 + yy * 4 + xx
@@ -93,16 +93,19 @@
         u, v = (u + a) % 4, (v + b) % 4
         return u, v, (expert_at(u, v, x), expert_at(u, y, v), expert_at(z, u, v))[c]
 
-    def main_rows(ref, c, u, v):
+    def nearest(i):
+        return jnp.where(i < 7, 0x8DF134C >> (4 * jnp.minimum(i, 6)), 0x6A9BE257 >> (4 * jnp.maximum(i - 7, 0))) & 15
+
+    def main_rows(ref, t, c, u, v):
         if c == 0:
-            return ref.at[u, v, :, :, cols[c]]
+            return ref.at[u, v, :, :, cols[t][c]]
         if c == 1:
-            return ref.at[u, :, v, :, cols[c]]
-        return ref.at[pl.ds(0, 4), u, v, :, cols[c]]
-
-    def tail_rows(ref, sides, c, u, v):
+            return ref.at[u, :, v, :, cols[t][c]]
+        return ref.at[pl.ds(0, 4), u, v, :, cols[t][c]]
+
+    def tail_rows(ref, sides, t, c, u, v):
         if c == 0:
-            return ref.at[4 + u // 2, (u % 2) * 2 + v // 2, pl.ds((v % 2) * 2, 2), :, cols[c]]
+            return ref.at[4 + u // 2, (u % 2) * 2 + v // 2, pl.ds((v % 2) * 2, 2), :, cols[t][c]]
         return sides[c].at[u * 4 + v]
 
     def remote(src, dst, s, r, who, core):
@@ -117,47 +120,78 @@
     plane_uv = ((z, y), (z, x), (y, x))
 
     barrier = pltpu.get_barrier_semaphore()
-    greeted = [(a, b, c) for a in range(4) for b in range(4) for c in range(4) if 0 in (a, b, c) and (a, b, c) != (0, 0, 0)]
-    for a, b, c in greeted:
-        who = expert_at((z + a) % 4, (y + b) % 4, (x + c) % 4)
-        pl.semaphore_signal(barrier, inc=1, device_id=(who, d), device_id_type=MESH)
+    for c in range(3):
+        for k in (2, 1, 3):
+            pl.semaphore_signal(barrier, inc=1, device_id=(line_peer(c, k)[1], d), device_id_type=MESH)
     pl.semaphore_signal(barrier, inc=1, device_id=(e, 1 - d), device_id_type=MESH)
 
-    for c in range(3):
-        pltpu.make_async_copy(tok.at[:, cols[c]], t4[c].at[here[c]], in_l.at[c]).start()
-    codes_in = pltpu.make_async_copy(cin, cinv, in_l.at[6])
-    codes_out = pltpu.make_async_copy(cout, coutv, in_l.at[7])
-    codes_in.start()
-    codes_out.start()
-    for c in range(3):
-        pltpu.make_async_copy(go.at[:, cols[c]], g4[c].at[here[c]], in_l.at[3 + c]).start()
+    small = [(ids, idv), (rw, rwv), (clin, clinv), (rgin, rginv), (clout, cloutv), (rgout, rgoutv), (cin, cinv), (cout, coutv)]
+    loads = [pltpu.make_async_copy(src, dst, in_l.at[6 + i]) for i, (src, dst) in enumerate(small)]
+    loads[0].start()
+    loads[1].start()
+    for c in range(3):
+        pltpu.make_async_copy(tok.at[:, cols[0][c]], t4[c].at[here[c]], in_l.at[c]).start()
+    for c in range(3):
+        pltpu.make_async_copy(go.at[:, cols[1][c]], g4[c].at[here[c]], in_l.at[3 + c]).start()
+    for load in loads[2:]:
+        load.start()
+    loads[0].wait()
+    loads[1].wait()
 
     row = iota((128, TOK), 0)
     chosen = jnp.zeros((128, TOK), F32)
     weight = jnp.zeros((128, TOK), F32)
     for k in range(8):
-        ident = ids[k : k + 1, :]
+        ident = idv[k : k + 1, :]
         chosen = chosen + jnp.where(row == ident, 1.0, 0.0)
-        weight = weight + jnp.where(row == ident + 64, rw[k : k + 1, :], 0.0)
+        weight = weight + jnp.where(row == ident + 64, rwv[k : k + 1, :], 0.0)
     earlier = jnp.where(iota((TOK, TOK), 0) < iota((TOK, TOK), 1), 1.0, 0.0).astype(BF)
     before = dot(chosen.astype(BF), earlier, 1, 0)
-    rank = jnp.where(chosen > 0.5, before, jnp.where(row < 64, -64.0, 0.0)) + weight
-    posw[...] = rank.T
-    for c in range(3):
-        pw4[c, here[c]] = posw[...]
-
-    ends = [sigmoid(clin[p, t]) * rgin[p, t] for p in range(2) for t in range(2)]
+    rank = jnp.where(chosen > 0.5, before, jnp.where(row < 64, -64.0, 0.0))
+    table = rank + weight
+    high = table.astype(BF).astype(F32)
+    left = table - high
+    mid = left.astype(BF).astype(F32)
+    low = left - mid
+    table = jnp.concatenate([high, jnp.concatenate([low[64:], mid[64:]], axis=0)], axis=1).astype(BF)
+    plans = []
+    for c in range(3):
+        s, i = iota((4, 32, 128), 0), iota((4, 32, 128), 1)
+        u, v = (i >> 2) & 3, i & 3
+        named = (expert_at(u, v, s), expert_at(u, s, v), expert_at(s, u, v))[c] + (i >> 4) * 64
+        plans.append(jnp.where(iota((4, 32, 128), 2) == named, 1.0, 0.0).reshape(128, 128))
+    plans = jnp.concatenate(plans, axis=0).astype(BF)
+    tab.reshape(384, 128)[...] = dot(plans, table, 1, 0).astype(BF)
+    for c in range(3):
+        pw4[c, here[c]] = tab[c * 4 + here[c]]
+
+    for c in range(3):
+        wait_bytes(t4[c].at[here[c]], in_l.at[c])
+        wait_bytes(g4[c].at[here[c]], in_l.at[3 + c])
+    pl.semaphore_wait(barrier, 10)
+
+    for k in (2, 1, 3):
+        for c in range(3):
+            at, who = line_peer(c, k)
+            remote(tab.at[c * 4 + at], pw4.at[c, here[c]], pw_s.at[c], pw_r.at[c], who, d).start()
+    for t, q4 in enumerate((t4, g4)):
+        for k in (2, 1, 3):
+            for c in range(3):
+                _, who = line_peer(c, k)
+                mine = q4[c].at[here[c]]
+                remote(mine, mine, ag_s.at[t, c], ag_r.at[t, c], who, d).start()
+
+    for load in loads[2:]:
+        load.wait()
+    ends = [sigmoid(clinv[p, t]) * rginv[p, t] for p in range(2) for t in range(2)]
     ends = join3(dot(split3(jnp.concatenate(ends, axis=0)), nibble_order(), 1, 0))
     for p in range(2):
         upgu[:, p * FF : (p + 1) * FF] = ends[p * 32 : p * 32 + 16]
         logu[:, p * FF : (p + 1) * FF] = ends[p * 32 + 16 : p * 32 + 32]
     for g in range(6):
-        end = sigmoid(clout[g]) * rgout[g]
+        end = sigmoid(cloutv[g]) * rgoutv[g]
         upo[g : g + 1, :] = end[0:1]
         loo[g : g + 1, :] = end[1:2]
-
-    codes_in.wait()
-    codes_out.wait()
 
     def dequant_in(g, carry):
         up = upgu[pl.ds(d * 8 + g, 1), :]
@@ -186,85 +220,67 @@
             shift = jnp.where(unit >= first, lo_half[g][None], shift)
         wd[k * 256 + r0 : k * 256 + r0 + 32, half] = (code * scale - shift).astype(BF)
 
-    for c in range(3):
-        wait_bytes(t4[c].at[here[c]], in_l.at[c])
-        wait_bytes(g4[c].at[here[c]], in_l.at[3 + c])
-    pl.semaphore_wait(barrier, len(greeted) + 1)
-
-    for k in (2, 1, 3):
-        for c in range(3):
-            _, who = line_peer(c, k)
-            remote(posw, pw4.at[c, here[c]], pw_s.at[c], pw_r.at[c], who, d).start()
-    for k in (2, 1, 3):
-        for c in range(3):
-            _, who = line_peer(c, k)
-            mine = t4[c].at[here[c]]
-            remote(mine, mine, ag_s.at[0, c], ag_r.at[0, c], who, d).start()
-    for k in (2, 1, 3):
-        for c in range(3):
-            _, who = line_peer(c, k)
-            mine = g4[c].at[here[c]]
-            remote(mine, mine, ag_s.at[1, c], ag_r.at[1, c], who, d).start()
-
     other = 1 - d
     wgu_half = wgu.at[pl.ds(pl.multiple_of(d * 1024, 1024), 1024), :]
     wd_half = wd.at[:, half]
     remote(wgu_half, wgu_half, wt_s.at[0], wt_r.at[0], e, other).start()
     remote(wd_half, wd_half, wt_s.at[1], wt_r.at[1], e, other).start()
 
-    def selector(c, first):
+    def selector(first):
         def rows(n):
-            q = iota((16, n, 128), 0)
-            u, v = q >> 2, q & 3
-            target = (u * 16 + v * 4 + x, u * 16 + y * 4 + v, z * 16 + u * 4 + v)[c]
-            return jnp.where(iota((16, n, 128), 2) == target + first, 1.0, 0.0).reshape(16 * n, 128)
+            hit = iota((16, n, 32), 2) == iota((16, n, 32), 0) + first
+            return jnp.where(hit, 1.0, 0.0).reshape(16 * n, 32)
 
         return jnp.concatenate([rows(32), rows(16)], axis=0).astype(BF)
 
+    first_half, second_half, either = selector(0), selector(16), selector(0) + selector(16)
     r = iota((16, 32, 256), 1)
     want_main = (r >> 3) * 16 + (r & 7) - 16 * (iota((16, 32, 256), 2) >> 6)
     r = iota((16, 16, 256), 1)
     want_tail = (r >> 2) * 16 + 8 + (r & 3) - 16 * (iota((16, 16, 256), 2) >> 6)
     wanted = jnp.concatenate([want_main.reshape(512, 256), want_tail.reshape(256, 256)], axis=0).astype(F32)
 
-    def spread(c, t, src, to):
+    def spread(t, src, to):
         def one(i, carry):
-            o = jnp.where(i < 6, 10 + i, i - 5)
-            u, v, who = plane_peer(c, o)
-            remote(src.at[u * 4 + v], to, sl_s.at[t, c], sl_r.at[t, c], who, d).start()
+            for c in range(3):
+                u, v, who = plane_peer(c, nearest(i))
+                remote(src[c].at[u * 4 + v], to(c), sl_s.at[t, c], sl_r.at[t, c], who, d).start()
             return carry
 
         lax.fori_loop(0, 15, one, 0)
-        pltpu.make_async_copy(src.at[plane_me[c]], to, sl_l.at[t, c]).start()
-
+        for c in range(3):
+            pltpu.make_async_copy(src[c].at[plane_me[c]], to(c), sl_l.at[t, c]).start()
+
+    above, below = [], []
     for c in range(3):
         wait_bytes(pw4.at[c, pl.ds(0, 3)], pw_r.at[c])
-        found = dot(selector(c, 0), pw4[c].reshape(256, 128).astype(BF), 1, 1)
+        heard = [pw4[c, s].astype(F32) for s in range(4)]
+        above.append(jnp.concatenate([v[:, :64] for v in heard], axis=1).astype(BF))
+        below.append(jnp.concatenate([v[:, 64:] for v in heard], axis=1).astype(BF))
+        found = dot(first_half, above[c], 1, 0)
         p4s[c] = jnp.where(found == wanted, 1.0, 0.0).astype(BF)
     for c in range(3):
         wait_bytes(t4[c].at[pl.ds(0, 3)], ag_r.at[0, c])
-        rows = dot(p4s[c, :512], t4[c][...].reshape(256, WIDTH[c]), 1, 0).astype(BF)
-        s_main[0][c].reshape(512, WIDTH[c])[...] = rows
-        spread(c, 0, s_main[0][c], main_rows(x5, c, *plane_uv[c]))
+        rows = dot(p4s[c, :512], t4[c][...].reshape(256, WIDTH[0][c]), 1, 0).astype(BF)
+        s_main[0][c].reshape(512, WIDTH[0][c])[...] = rows
+    spread(0, s_main[0], lambda c: main_rows(x5, 0, c, *plane_uv[c]))
     slot_weights = []
     for c in range(3):
-        parts = split3(pw4[c].reshape(256, 128))
-        named = dot(selector(c, 64), parts, 1, 1)
-        named = (named[:, 512:] + named[:, 256:512]) + named[:, :256]
+        named = dot(either, below[c], 1, 0) + dot(second_half, above[c], 1, 0)
         slot_weights.append(jnp.sum(p4s[c].astype(F32) * named, axis=1, keepdims=True))
     for c in range(3):
         wait_bytes(g4[c].at[pl.ds(0, 3)], ag_r.at[1, c])
-        rows = dot(p4s[c, :512], g4[c][...].reshape(256, WIDTH[c]), 1, 0)
-        s_main[1][c].reshape(512, WIDTH[c])[...] = (slot_weights[c][:512] * rows).astype(BF)
-        spread(c, 1, s_main[1][c], main_rows(d5, c, *plane_uv[c]))
-    for c in range(3):
-        rows = dot(p4s[c, 512:], t4[c][...].reshape(256, WIDTH[c]), 1, 0).astype(BF)
-        s_tail[0][c].reshape(256, WIDTH[c])[...] = rows
-        spread(c, 2, s_tail[0][c], tail_rows(x5, xe, c, *plane_uv[c]))
-    for c in range(3):
-        rows = dot(p4s[c, 512:], g4[c][...].reshape(256, WIDTH[c]), 1, 0)
-        s_tail[1][c].reshape(256, WIDTH[c])[...] = (slot_weights[c][512:] * rows).astype(BF)
-        spread(c, 3, s_tail[1][c], tail_rows(d5, de, c, *plane_uv[c]))
+        rows = dot(p4s[c, :512], g4[c][...].reshape(256, WIDTH[1][c]), 1, 0)
+        s_main[1][c].reshape(512, WIDTH[1][c])[...] = (slot_weights[c][:512] * rows).astype(BF)
+    spread(1, s_main[1], lambda c: main_rows(d5, 1, c, *plane_uv[c]))
+    for c in range(3):
+        rows = dot(p4s[c, 512:], t4[c][...].reshape(256, WIDTH[0][c]), 1, 0).astype(BF)
+        s_tail[0][c].reshape(256, WIDTH[0][c])[...] = rows
+    spread(2, s_tail[0], lambda c: tail_rows(x5, xe, 0, c, *plane_uv[c]))
+    for c in range(3):
+        rows = dot(p4s[c, 512:], g4[c][...].reshape(256, WIDTH[1][c]), 1, 0)
+        s_tail[1][c].reshape(256, WIDTH[1][c])[...] = (slot_weights[c][512:] * rows).astype(BF)
+    spread(3, s_tail[1], lambda c: tail_rows(d5, de, 1, c, *plane_uv[c]))
 
     def moved(v, c):
         if c == 1:
@@ -276,11 +292,11 @@
             wait_bytes(src[c].at[pl.ds(0, 15)], sl_r.at[t, c])
             wait_bytes(src[c].at[0], sl_l.at[t, c])
 
-    def order_tail(to, sides):
+    def order_tail(to, sides, t):
         for c in (1, 2):
             order = jnp.where(iota((256, 256), 0) == moved(iota((256, 256), 1), c), 1.0, 0.0).astype(BF)
-            to.reshape(768, D)[512:768, FIRST[c] : FIRST[c] + WIDTH[c]] = dot(
-                order, sides[c][...].reshape(256, WIDTH[c]), 1, 0
+            to.reshape(768, D)[512:768, FIRST[t][c] : FIRST[t][c] + WIDTH[t][c]] = dot(
+                order, sides[c][...].reshape(256, WIDTH[t][c]), 1, 0
             ).astype(BF)
 
     def forward(i, carry):
@@ -304,17 +320,15 @@
         return carry
 
     def give_back(t, dst, rows_of):
+        def one(i, carry):
+            for c in range(3):
+                u, v, who = plane_peer(c, nearest(i))
+                remote(rows_of(c, u, v), dst[c].at[plane_me[c]], rt_s.at[t, c], rt_r.at[t, c], who, d).start()
+            return carry
+
+        lax.fori_loop(0, 15, one, 0)
         for c in range(3):
-            to = dst[c].at[plane_me[c]]
-
-            def one(i, carry, c=c, to=to):
-                o = jnp.where(i < 6, 10 + i, i - 5)
-                u, v, who = plane_peer(c, o)
-                remote(rows_of(c, u, v), to, rt_s.at[t, c], rt_r.at[t, c], who, d).start()
-                return carry
-
-            lax.fori_loop(0, 15, one, 0)
-            pltpu.make_async_copy(rows_of(c, *plane_uv[c]), to, rt_l.at[t, c]).start()
+            pltpu.make_async_copy(rows_of(c, *plane_uv[c]), dst[c].at[plane_me[c]], rt_l.at[t, c]).start()
 
     wait_bytes(wgu_half, wt_r.at[0])
     wait_bytes(wd_half, wt_r.at[1])
@@ -322,20 +336,20 @@
     lax.fori_loop(0, 2, forward, 0)
     arrived(1, s_main[1])
     lax.fori_loop(0, 2, backward, 0)
-    give_back(0, r_main, lambda c, u, v: main_rows(g5, c, u, v))
+    give_back(0, r_main, lambda c, u, v: main_rows(g5, 2, c, u, v))
 
     arrived(2, s_tail[0])
-    order_tail(x5, xe)
+    order_tail(x5, xe, 0)
     lax.fori_loop(2, 3, forward, 0)
     arrived(3, s_tail[1])
-    order_tail(d5, de)
+    order_tail(d5, de, 1)
     lax.fori_loop(2, 3, backward, 0)
     for c in (1, 2):
         order = jnp.where(moved(iota((256, 256), 0), c) == iota((256, 256), 1), 1.0, 0.0).astype(BF)
-        ge[c].reshape(256, WIDTH[c])[...] = dot(
-            order, g5.reshape(768, D)[512:768, FIRST[c] : FIRST[c] + WIDTH[c]], 1, 0
+        ge[c].reshape(256, WIDTH[2][c])[...] = dot(
+            order, g5.reshape(768, D)[512:768, FIRST[2][c] : FIRST[2][c] + WIDTH[2][c]], 1, 0
         ).astype(BF)
-    give_back(1, r_tail, lambda c, u, v: tail_rows(g5, ge, c, u, v))
+    give_back(1, r_tail, lambda c, u, v: tail_rows(g5, ge, 2, c, u, v))
 
     def sums_in(j, carry):
         wide = pl.ds(pl.multiple_of(j * 512, 512), 512)
@@ -386,28 +400,28 @@
     plain = join3(dot(split3(jnp.concatenate(totals, axis=0)), nibble_order(), 1, 1))
     for p in range(2):
         for t in range(2):
-            sig = sigmoid(clin[p, t, share, :])
+            sig = sigmoid(clinv[p, t, share, :])
             total = plain[(p * 2 + t) * 8 : (p * 2 + t) * 8 + 8]
-            o_in[0, p, t] = total * rgin[p, t, share, :] * sig * (1.0 - sig)
+            o_in[0, p, t] = total * rginv[p, t, share, :] * sig * (1.0 - sig)
     wait_bytes(rbo, sm_r.at[1])
     span = upo[:, half] + loo[:, half]
     upper_out = (sbo[d, 0] + rbo[0])[:6] / span
     lower_out = upper_out - (sbo[d, 1] + rbo[1])[:6]
     for g in range(6):
-        sig = sigmoid(clout[g, :, half])
+        sig = sigmoid(cloutv[g, :, half])
         total = jnp.concatenate([upper_out[g : g + 1], lower_out[g : g + 1]], axis=0)
-        o_out[g] = total * rgout[g, :, half] * sig * (1.0 - sig)
+        o_out[g] = total * rgoutv[g, :, half] * sig * (1.0 - sig)
 
     sums = []
     for c in range(3):
-        wait_bytes(s_main[0][c].at[pl.ds(0, 15)], rt_r.at[0, c])
-        wait_bytes(s_main[0][c].at[0], rt_l.at[0, c])
-        sums.append(dot(p4s[c, :512], r_main[c].reshape(512, WIDTH[c])[...], 0, 0))
-    for c in range(3):
-        wait_bytes(s_tail[0][c].at[pl.ds(0, 15)], rt_r.at[1, c])
-        wait_bytes(s_tail[0][c].at[0], rt_l.at[1, c])
-        total = sums[c] + dot(p4s[c, 512:], r_tail[c].reshape(256, WIDTH[c])[...], 0, 0)
-        part[c][...] = total.astype(BF).reshape(4, TOK, WIDTH[c])
+        wait_bytes(r_main[c].at[pl.ds(0, 15)], rt_r.at[0, c])
+        wait_bytes(r_main[c].at[0], rt_l.at[0, c])
+        sums.append(dot(p4s[c, :512], r_main[c].reshape(512, WIDTH[2][c])[...], 0, 0))
+    for c in range(3):
+        wait_bytes(r_tail[c].at[pl.ds(0, 15)], rt_r.at[1, c])
+        wait_bytes(r_tail[c].at[0], rt_l.at[1, c])
+        total = sums[c] + dot(p4s[c, 512:], r_tail[c].reshape(256, WIDTH[2][c])[...], 0, 0)
+        part[c][...] = total.astype(BF).reshape(4, TOK, WIDTH[2][c])
         for k in (2, 1, 3):
             s, who = line_peer(c, k)
             remote(part[c].at[s], got[c].at[here[c]], pt_s.at[c], pt_r.at[c], who, d).start()
@@ -417,7 +431,7 @@
         for k in (1, 2, 3):
             s, _ = line_peer(c, k)
             total = total + got[c][s].astype(F32)
-        o_tok[:, cols[c]] = total.astype(BF)
+        o_tok[:, cols[2][c]] = total.astype(BF)
 
     for c in range(3):
         wait_bytes(pw4.at[c, pl.ds(0, 3)], pw_s.at[c])
@@ -426,8 +440,8 @@
         for t in range(2):
             wait_bytes(s_main[t][c].at[pl.ds(0, 15)], sl_s.at[t, c])
             wait_bytes(s_tail[t][c].at[pl.ds(0, 15)], sl_s.at[2 + t, c])
-        wait_bytes(s_main[0][c].at[pl.ds(0, 15)], rt_s.at[0, c])
-        wait_bytes(s_tail[0][c].at[pl.ds(0, 15)], rt_s.at[1, c])
+        wait_bytes(r_main[c].at[pl.ds(0, 15)], rt_s.at[0, c])
+        wait_bytes(r_tail[c].at[pl.ds(0, 15)], rt_s.at[1, c])
         wait_bytes(got[c].at[pl.ds(0, 3)], pt_s.at[c])
     wait_bytes(wgu_half, wt_s.at[0])
     wait_bytes(wd_half, wt_s.at[1])
@@ -446,18 +460,20 @@
         return pltpu.VMEM(shape, t)
 
     dma = pltpu.SemaphoreType.DMA
-    scratch = [vm(TOK, 128, t=F32)]
-    scratch += [vm(4, TOK, w) for w in WIDTH] * 2 + [vm(3, 4, TOK, 128, t=F32)]
-    scratch += [vm(16, 4, 8, w) for w in WIDTH] * 2 + [vm(16, 2, 8, w) for w in WIDTH] * 2
+    tok_w, slope_w, back_w = WIDTH
+    scratch = [vm(12, 32, 128)]
+    scratch += [vm(4, TOK, w) for w in tok_w + slope_w] + [vm(3, 4, 32, 128)]
+    scratch += [vm(16, 4, 8, w) for w in tok_w + slope_w] + [vm(16, 2, 8, w) for w in tok_w + slope_w]
     scratch += [vm(6, 4, 4, 8, D)] * 3
-    scratch += [vm(16, 2, 8, w) for w in WIDTH[1:]] * 3
-    scratch += [vm(16, 4, 8, w) for w in WIDTH] + [vm(16, 2, 8, w) for w in WIDTH] + [vm(3, 768, 256)]
+    scratch += [vm(16, 2, 8, w) for w in tok_w[1:] + slope_w[1:] + back_w[1:]]
+    scratch += [vm(16, 4, 8, w) for w in back_w] + [vm(16, 2, 8, w) for w in back_w] + [vm(3, 768, 256)]
     scratch += [vm(D, 2 * FF), vm(FF, D), vm(16, 2 * FF, t=F32), vm(16, 2 * FF, t=F32), vm(6, D, t=F32), vm(6, D, t=F32)]
-    scratch += [vm(2, 1024, 256, t=I32), vm(256, 1024, t=I32)]
+    scratch += [vm(2, 1024, 256, t=I32), vm(256, 1024, t=I32), vm(8, TOK, t=I32), vm(8, TOK, t=F32)]
+    scratch += [vm(2, 2, 16, FF, t=F32)] * 2 + [vm(6, 2, D, t=F32)] * 2
     scratch += [vm(768, FF), vm(768, 2 * FF), vm(768, FF, t=F32), vm(768, FF, t=F32)]
-    scratch += [vm(4, TOK, w) for w in WIDTH] * 2
+    scratch += [vm(4, TOK, w) for w in back_w] * 2
     scratch += [vm(2, 2, 8, 2 * FF, t=F32), vm(2, 2, 8, 1024, t=F32), vm(2, 8, 2 * FF, t=F32), vm(2, 8, 1024, t=F32)]
-    scratch += [dma((8,)), dma((2, 3)), dma((2, 3)), dma((3,)), dma((3,)), dma((4, 3)), dma((4, 3)), dma((4, 3))]
+    scratch += [dma((14,)), dma((2, 3)), dma((2, 3)), dma((3,)), dma((3,)), dma((4, 3)), dma((4, 3)), dma((4, 3))]
     scratch += [dma((2, 3)), dma((2, 3)), dma((2, 3)), dma((3,)), dma((3,)), dma((2,)), dma((2,)), dma((2,)), dma((2,))]
     args = (
         tokens, grad_out, expert_ids.T, router_weights.T, codes_in[0], codes_out[0],
@@ -471,15 +487,15 @@
     )
     found = pl.pallas_call(
         kernel,
-        out_shape=results,
-        in_specs=[anywhere, anywhere, vmem, vmem, anywhere, anywhere, vmem, vmem, vmem, vmem],
+        out_shape=tuple(pltpu.VMEM(v.shape, v.dtype) for v in results),
+        in_specs=[anywhere] * len(args),
         out_specs=(vmem,) * 3,
         scratch_shapes=scratch,
         compiler_params=pltpu.CompilerParams(collective_id=0, has_side_effects=True, vmem_limit_bytes=62 << 20),
     )(*args)
     grad_tokens, grad_in, grad_out_clip = pl.pallas_call(
         hand_out, out_shape=results, in_specs=[vmem] * 3, out_specs=(vmem,) * 3
-    )(*found)
+    )(*(pltpu.with_memory_space_constraint(v, pltpu.VMEM) for v in found))
     return grad_tokens, grad_in, grad_out_clip.transpose(1, 0, 2)[None]
 
 

time: 103 us -> 94.5 us (0.917); the launches traced: 102 us -> 94.3 us
  Pallas kernels: 101 us -> 93.7 us
    pallas_call x1, Pallas kernels: 99.2 us -> 92.9 us  [body(): pl.pallas_call(kernel, out_shape=tuple((pltpu.VMEM(v.shape, v.dtype) for...]
where the time goes in v2:
time: 94.5 us; the launch traced here: 94.3 us
  Pallas kernels  93.7 us (99%)
    pallas_call x1, Pallas kernels, body(): pl.pallas_call(kernel, out_shape=tuple((pltpu.VMEM(v.shape, v.dtype) for...  92.9 us

profile of v2, /device:TPU:0, one launch (start us, length us, event | category | flops | bytes accessed | tf_op | source)
XLA Modules:
  0.0 94.3 jit_solution(6204639615300104172)
XLA Ops:
  0.6 92.9 %shard_map.121 = (bf16[64,2048]{1,0:T(8,128)(2,1)S(1)}, f32[1,2,2,8,768]{4,3,2,1,0:T(8,128)S(1)}, f32[6,2,1024]{2,1,0:T(2,128)S(1)}) custom-call(bf16[64,2048]{1,0:T(8,128)(2,1)} %tok.1, bf16[64,2048]{1,0:T(8,128)(2,1)} %go.1, s32[8,64]{1,0:T(8,128)} %bitcast.21, f32[8,64]{1,0:T(8,128)} %bitcast.22, s32[2,1024,256]{2,1,0:T(8,128)} %bitcast.15, ...), custom_call_target="tpu_custom_call" | custom-call | tf_op jit(solution)/shard_map/pallas_call | solution.py:488
  93.6 0.8 shard_map.122

commit v3 on v2

--- a/solution.py
+++ b/solution.py
@@ -64,7 +64,7 @@
     tab, t4a, t4b, t4c, g4a, g4b, g4c, pw4,
     sma, smb, smc, dma_, dmb, dmc, sxa, sxb, sxc, dxa, dxb, dxc,
     x5, d5, g5, xeb, xec, deb, dec, geb, gec,
-    rma, rmb, rmc, rxa, rxb, rxc, p4s,
+    rma, rmb, rmc, rxa, rxb, rxc, p4s, p4t, ta, tb, tc,
     wgu, wd, upgu, logu, upo, loo, cinv, coutv, idv, rwv, clinv, rginv, cloutv, rgoutv,
     hid, ggu, fac, act, qa, qb, qc, ha, hb, hc,
     sbi, sbo, rbi, rbo,
@@ -240,16 +240,17 @@
     want_tail = (r >> 2) * 16 + 8 + (r & 3) - 16 * (iota((16, 16, 256), 2) >> 6)
     wanted = jnp.concatenate([want_main.reshape(512, 256), want_tail.reshape(256, 256)], axis=0).astype(F32)
 
-    def spread(t, src, to):
+    def spread(t, src, to, first=0, last=15, ranges=(0, 1, 2)):
         def one(i, carry):
-            for c in range(3):
+            for c in ranges:
                 u, v, who = plane_peer(c, nearest(i))
                 remote(src[c].at[u * 4 + v], to(c), sl_s.at[t, c], sl_r.at[t, c], who, d).start()
             return carry
 
-        lax.fori_loop(0, 15, one, 0)
-        for c in range(3):
-            pltpu.make_async_copy(src[c].at[plane_me[c]], to(c), sl_l.at[t, c]).start()
+        lax.fori_loop(first, last, one, 0)
+        if last == 15:
+            for c in ranges:
+                pltpu.make_async_copy(src[c].at[plane_me[c]], to(c), sl_l.at[t, c]).start()
 
     above, below = [], []
     for c in range(3):
@@ -263,7 +264,8 @@
         wait_bytes(t4[c].at[pl.ds(0, 3)], ag_r.at[0, c])
         rows = dot(p4s[c, :512], t4[c][...].reshape(256, WIDTH[0][c]), 1, 0).astype(BF)
         s_main[0][c].reshape(512, WIDTH[0][c])[...] = rows
-    spread(0, s_main[0], lambda c: main_rows(x5, 0, c, *plane_uv[c]))
+        spread(0, s_main[0], lambda c: main_rows(x5, 0, c, *plane_uv[c]), 0, 4, (c,))
+    spread(0, s_main[0], lambda c: main_rows(x5, 0, c, *plane_uv[c]), 4)
     slot_weights = []
     for c in range(3):
         named = dot(either, below[c], 1, 0) + dot(second_half, above[c], 1, 0)
@@ -330,6 +332,8 @@
         for c in range(3):
             pltpu.make_async_copy(rows_of(c, *plane_uv[c]), dst[c].at[plane_me[c]], rt_l.at[t, c]).start()
 
+    for c in range(3):
+        p4t[c] = p4s[c].T
     wait_bytes(wgu_half, wt_r.at[0])
     wait_bytes(wd_half, wt_r.at[1])
     arrived(0, s_main[0])
@@ -412,15 +416,15 @@
         total = jnp.concatenate([upper_out[g : g + 1], lower_out[g : g + 1]], axis=0)
         o_out[g] = total * rgoutv[g, :, half] * sig * (1.0 - sig)
 
-    sums = []
+    sums = (ta, tb, tc)
     for c in range(3):
         wait_bytes(r_main[c].at[pl.ds(0, 15)], rt_r.at[0, c])
         wait_bytes(r_main[c].at[0], rt_l.at[0, c])
-        sums.append(dot(p4s[c, :512], r_main[c].reshape(512, WIDTH[2][c])[...], 0, 0))
+        sums[c][...] = dot(p4t[c, :, :512], r_main[c].reshape(512, WIDTH[2][c])[...], 1, 0)
     for c in range(3):
         wait_bytes(r_tail[c].at[pl.ds(0, 15)], rt_r.at[1, c])
         wait_bytes(r_tail[c].at[0], rt_l.at[1, c])
-        total = sums[c] + dot(p4s[c, 512:], r_tail[c].reshape(256, WIDTH[2][c])[...], 0, 0)
+        total = sums[c][...] + dot(p4t[c, :, 512:], r_tail[c].reshape(256, WIDTH[2][c])[...], 1, 0)
         part[c][...] = total.astype(BF).reshape(4, TOK, WIDTH[2][c])
         for k in (2, 1, 3):
             s, who = line_peer(c, k)
@@ -466,7 +470,8 @@
     scratch += [vm(16, 4, 8, w) for w in tok_w + slope_w] + [vm(16, 2, 8, w) for w in tok_w + slope_w]
     scratch += [vm(6, 4, 4, 8, D)] * 3
     scratch += [vm(16, 2, 8, w) for w in tok_w[1:] + slope_w[1:] + back_w[1:]]
-    scratch += [vm(16, 4, 8, w) for w in back_w] + [vm(16, 2, 8, w) for w in back_w] + [vm(3, 768, 256)]
+    scratch += [vm(16, 4, 8, w) for w in back_w] + [vm(16, 2, 8, w) for w in back_w] + [vm(3, 768, 256), vm(3, 256, 768)]
+    scratch += [vm(256, w, t=F32) for w in back_w]
     scratch += [vm(D, 2 * FF), vm(FF, D), vm(16, 2 * FF, t=F32), vm(16, 2 * FF, t=F32), vm(6, D, t=F32), vm(6, D, t=F32)]
     scratch += [vm(2, 1024, 256, t=I32), vm(256, 1024, t=I32), vm(8, TOK, t=I32), vm(8, TOK, t=F32)]
     scratch += [vm(2, 2, 16, FF, t=F32)] * 2 + [vm(6, 2, D, t=F32)] * 2

time: 94.5 us -> 93.5 us (0.989)
    pallas_call x1, Pallas kernels: 92.9 us -> 92 us  [body(): pl.pallas_call(kernel, out_shape=tuple((pltpu.VMEM(v.shape, v.dtype) for...]
where the time goes in v3:
time: 93.5 us; the launch traced here: 93.4 us
  Pallas kernels  92.8 us (99%)
    pallas_call x1, Pallas kernels, body(): pl.pallas_call(kernel, out_shape=tuple((pltpu.VMEM(v.shape, v.dtype) for...  92 us

profile of v3, /device:TPU:0, one launch (start us, length us, event | category | flops | bytes accessed | tf_op | source)
XLA Modules:
  0.0 93.4 jit_solution(7373582911447671890)
XLA Ops:
  0.6 92.0 %shard_map.121 = (bf16[64,2048]{1,0:T(8,128)(2,1)S(1)}, f32[1,2,2,8,768]{4,3,2,1,0:T(8,128)S(1)}, f32[6,2,1024]{2,1,0:T(2,128)S(1)}) custom-call(bf16[64,2048]{1,0:T(8,128)(2,1)} %tok.1, bf16[64,2048]{1,0:T(8,128)(2,1)} %go.1, s32[8,64]{1,0:T(8,128)} %bitcast.21, f32[8,64]{1,0:T(8,128)} %bitcast.22, s32[2,1024,256]{2,1,0:T(8,128)} %bitcast.15, ...), custom_call_target="tpu_custom_call" | custom-call | tf_op jit(solution)/shard_map/pallas_call | solution.py:493
  92.6 0.8 shard_map.122

commit v4 on v3

--- a/solution.py
+++ b/solution.py
@@ -87,6 +87,9 @@
         s = (here[c] + k) % 4
         return s, (expert_at(z, y, s), expert_at(z, s, x), expert_at(s, y, x))[c]
 
+    def pieces(k):
+        return [pl.ds(0, TOK)] if k != 2 else [pl.ds(0, TOK // 2), pl.ds(TOK // 2, TOK // 2)]
+
     def plane_peer(c, o):
         a, b = o // 4, o % 4
         u, v = ((z, y), (z, x), (y, x))[c]
@@ -178,8 +181,9 @@
         for k in (2, 1, 3):
             for c in range(3):
                 _, who = line_peer(c, k)
-                mine = q4[c].at[here[c]]
-                remote(mine, mine, ag_s.at[t, c], ag_r.at[t, c], who, d).start()
+                for rows in pieces(k):
+                    mine = q4[c].at[here[c], rows]
+                    remote(mine, mine, ag_s.at[t, c], ag_r.at[t, c], who, d).start()
 
     for load in loads[2:]:
         load.wait()
@@ -428,7 +432,8 @@
         part[c][...] = total.astype(BF).reshape(4, TOK, WIDTH[2][c])
         for k in (2, 1, 3):
             s, who = line_peer(c, k)
-            remote(part[c].at[s], got[c].at[here[c]], pt_s.at[c], pt_r.at[c], who, d).start()
+            for rows in pieces(k):
+                remote(part[c].at[s, rows], got[c].at[here[c], rows], pt_s.at[c], pt_r.at[c], who, d).start()
     for c in range(3):
         wait_bytes(got[c].at[pl.ds(0, 3)], pt_r.at[c])
         total = part[c][here[c]].astype(F32)
@@ -453,10 +458,14 @@
     wait_bytes(sbo_out, sm_s.at[1])
 
 
-def hand_out(a, b, c, to_a, to_b, to_c):
-    to_a[...] = a[...]
-    to_b[...] = b[...]
-    to_c[...] = c[...]
+def hand_out(a, b, c, to_a, to_b, to_c, sems):
+    copies = [
+        pltpu.make_async_copy(src, dst, sems.at[i]) for i, (src, dst) in enumerate(((a, to_a), (b, to_b), (c, to_c)))
+    ]
+    for copy in copies:
+        copy.start()
+    for copy in copies:
+        copy.wait()
 
 
 def body(tokens, grad_out, expert_ids, router_weights, codes_in, codes_out, clip_in, range_in, clip_out, range_out):
@@ -499,7 +508,7 @@
         compiler_params=pltpu.CompilerParams(collective_id=0, has_side_effects=True, vmem_limit_bytes=62 << 20),
     )(*args)
     grad_tokens, grad_in, grad_out_clip = pl.pallas_call(
-        hand_out, out_shape=results, in_specs=[vmem] * 3, out_specs=(vmem,) * 3
+        hand_out, out_shape=results, in_specs=[vmem] * 3, out_specs=(anywhere,) * 3, scratch_shapes=[dma((3,))]
     )(*(pltpu.with_memory_space_constraint(v, pltpu.VMEM) for v in found))
     return grad_tokens, grad_in, grad_out_clip.transpose(1, 0, 2)[None]
 

time: 93.5 us -> 93.7 us (level)
  no operation moved by 1% of the time
where the time goes in v4:
time: 93.7 us; the launch traced here: 93.6 us
  Pallas kernels  92.8 us (99%)
    pallas_call x1, Pallas kernels, body(): pl.pallas_call(kernel, out_shape=tuple((pltpu.VMEM(v.shape, v.dtype) for...  92 us

profile of v4, /device:TPU:0, one launch (start us, length us, event | category | flops | bytes accessed | tf_op | source)
XLA Modules:
  0.0 93.6 jit_solution(960120807070366266)
XLA Ops:
  0.6 92.0 %shard_map.121 = (bf16[64,2048]{1,0:T(8,128)(2,1)S(1)}, f32[1,2,2,8,768]{4,3,2,1,0:T(8,128)S(1)}, f32[6,2,1024]{2,1,0:T(2,128)S(1)}) custom-call(bf16[64,2048]{1,0:T(8,128)(2,1)} %tok.1, bf16[64,2048]{1,0:T(8,128)(2,1)} %go.1, s32[8,64]{1,0:T(8,128)} %bitcast.21, f32[8,64]{1,0:T(8,128)} %bitcast.22, s32[2,1024,256]{2,1,0:T(8,128)} %bitcast.15, ...), custom_call_target="tpu_custom_call" | custom-call | tf_op jit(solution)/shard_map/pallas_call | solution.py:502
  92.6 0.8 shard_map.122
